TPU v7x, 512 devices: a whole 4x8x8 slice. The times are simulated.
512 devices in a mesh: leaf: 16 (over y, core), blk: 32 (over z, x).
Axes of the slice: x: 4, y: 8, z: 8, core: 2. Of those that a mesh axis runs over, the one named last changes fastest.
Arguments:
- adjoint_rhs: float32 [128, 128, 64], P('leaf'), may hold values from -6 to 6
- diag_inverse: float32 [128, 128, 128], P('leaf'), may hold values from -1 to 2
- blocks: float32 [16, 32, 32, 128, 128], P('leaf', 'blk'), may hold values from -0.03125 to 0.03125
- block_rows: int32 [16, 32, 32], P('leaf', 'blk'), may hold values from 0 to 127, as said below
- block_cols: int32 [16, 32, 32], P('leaf', 'blk'), may hold values from 0 to 7
- block_count: int32 [16, 32], P('leaf', 'blk'), may hold values from 0 to 32, as said below
- node_level: int32 [16], replicated, may hold values from 0 to 3, as said below
Outputs:
- adjoint_solution: float32 [128, 128, 64], P('leaf')
Inputs may be any that keep to these rules, and one draw needn't show every extreme that they name: `node_level`: exactly one node has level 0, and every level up to 3 is held by some node. `block_rows`: every live slot names a block row of a node whose level is lower than that of the slot's own node. `block_count`: the node of level 0 has no live slots; every other node has one device with exactly 32 live slots.
All inputs are finite; a program needn't handle non-finite values.
Results may differ from a plain program's by a relative error of at most 0.0003.
Values sent between devices are 32-bit elements; how exact they have to be, the bound alone decides.
A program may use at most 64 MiB of HBM per device.

v0:
```python
import jax
import jax.numpy as jnp
from jax import lax
from jax.sharding import PartitionSpec as P

LEVELS = 4


def accumulate(solved_all, tiles, row_ids, col_ids, trip_count, partial_shape):

    def add_tile(slot_at, partial_value):
        tile = lax.dynamic_index_in_dim(tiles, slot_at, 0, keepdims=False)
        row_at = lax.dynamic_index_in_dim(row_ids, slot_at, 0, keepdims=False)
        col_at = lax.dynamic_index_in_dim(col_ids, slot_at, 0, keepdims=False)
        panel_row = lax.dynamic_index_in_dim(solved_all, row_at, 0, keepdims=False)
        product = lax.dot_general(
            tile, panel_row, (((0,), (0,)), ((), ())), precision=lax.Precision.HIGHEST
        )
        current = lax.dynamic_index_in_dim(partial_value, col_at, 0, keepdims=False)
        return lax.dynamic_update_index_in_dim(partial_value, current + product, col_at, 0)

    return lax.fori_loop(0, trip_count, add_tile, jnp.zeros(partial_shape, jnp.float32))


def body(adjoint_rhs, diag_inverse, blocks, block_rows, block_cols, block_count, node_level):
    per_node, width, columns = adjoint_rhs.shape
    capacity = blocks.shape[2]
    leaves = lax.axis_size("leaf")
    my_depth = lax.dynamic_index_in_dim(node_level, lax.axis_index("leaf"), 0, keepdims=False)
    tiles = blocks.reshape(capacity, width, width)
    row_ids = block_rows.reshape(capacity)
    col_ids = block_cols.reshape(capacity)
    live_count = block_count.reshape(())
    solved_all = jnp.zeros((leaves * per_node, width, columns), jnp.float32)
    own_solution = jnp.zeros_like(adjoint_rhs)
    for section_level in range(LEVELS):
        active = my_depth == section_level
        trip_count = jnp.where(active, live_count, 0)
        partial_value = accumulate(
            solved_all, tiles, row_ids, col_ids, trip_count, (per_node, width, columns)
        )
        summed = lax.psum(partial_value, "blk")
        updated = jnp.einsum(
            "cij,cjk->cik", diag_inverse, adjoint_rhs - summed, precision=lax.Precision.HIGHEST
        )
        own_solution = jnp.where(active, updated, own_solution)
        if section_level + 1 < LEVELS:
            solved_all = lax.all_gather(own_solution, "leaf", axis=0, tiled=True)
    return own_solution


def solution(mesh):
    in_specs = (
        P("leaf", None, None),
        P("leaf", None, None),
        P("leaf", "blk", None, None, None),
        P("leaf", "blk", None),
        P("leaf", "blk", None),
        P("leaf", "blk"),
        P(),
    )
    out_specs = P("leaf", None, None)
    return jax.shard_map(body, mesh=mesh, in_specs=in_specs, out_specs=out_specs, check_vma=False)
```

profile of v0, /device:TPU:1, one launch (start us, length us, event | category | flops | bytes accessed | tf_op | source)
XLA Modules:
  0.0 1504.1 jit_solution(4455952233501976158)
XLA Ops:
  6.5 0.0 copy-start
  6.5 0.0 all-reduce.5.cloned.1.call-start
  7.3 1.3 dynamic_slice.67
  9.3 0.0 copy-start.3
  9.3 0.7 copy-done.3
  10.0 0.0 all-reduce.5.cloned.1.call-update
  10.0 0.0 all-gather.4.cloned.1.call-start
  10.0 157.3 %all-reduce.5.cloned.1.call-done = f32[8,128,64]{1,2,0:T(8,128)} async-done(((f32[8,128,64]{1,2,0:T(8,128)}), f32[8,128,64]{1,2,0:T(8,128)}) %all-reduce.5.cloned.1.call-update) | async-done | bytes 262160 | tf_op jit(solution)/shard_map/psum | solution.py:42
  167.4 0.0 copy-done
  167.4 2.8 fusion.31
  170.2 0.0 all-gather.4.cloned.1.call-update
  170.3 0.0 all-reduce.7.cloned.1.call-start
  170.9 45.4 %all-gather.4.cloned.1.call-done = f32[128,128,64]{1,2,0:T(8,128)} async-done(((f32[8,128,64]{1,2,0:T(8,128)}), f32[128,128,64]{1,2,0:T(8,128)}) %all-gather.4.cloned.1.call-update) | async-done | bytes 4194320 | tf_op jit(solution)/shard_map/all_gather | solution.py:48
  216.4 0.0 copy-start.4
  216.4 0.7 copy-done.4
  217.1 0.0 all-reduce.7.cloned.1.call-update
  217.1 0.0 all-gather.6.cloned.1.call-start
  217.2 397.0 %all-reduce.7.cloned.1.call-done = f32[8,128,64]{1,2,0:T(8,128)} async-done(((f32[8,128,64]{1,2,0:T(8,128)}), f32[8,128,64]{1,2,0:T(8,128)}) %all-reduce.7.cloned.1.call-update) | async-done | bytes 262160 | tf_op jit(solution)/shard_map/psum | solution.py:42
  614.2 0.0 copy-done.1
  614.2 2.9 fusion.30
  617.0 0.0 all-gather.6.cloned.1.call-update
  617.0 0.0 all-reduce.9.cloned.1.call-start
  617.7 45.4 %all-gather.6.cloned.1.call-done = f32[128,128,64]{1,2,0:T(8,128)} async-done(((f32[8,128,64]{1,2,0:T(8,128)}), f32[128,128,64]{1,2,0:T(8,128)}) %all-gather.6.cloned.1.call-update) | async-done | bytes 4194320 | tf_op jit(solution)/shard_map/all_gather | solution.py:48
  663.2 69.7 %while.43 = (s32[]{:T(128)}, f32[8,128,64]{1,2,0:T(8,128)S(1)}, s32[]{:T(128)}, s32[32]{0:T(128)}, f32[32,128,128]{2,1,0:T(8,128)}, /*index=5*/s32[32]{0:T(128)}...) while((s32[]{:T(128)}, f32[8,128,64]{1,2,0:T(8,128)S(1)}, ...), condition=%wide.region_7.8_spmd, body=%wide.region_6.7_spmd.sunk | while | flops 12591115 | bytes 229635 | solution.py:22
  663.2 1.3 dynamic_slice.129
  666.6 1.3 dynamic_slice.130
  669.9 1.0 fusion.60
  671.0 1.3 dynamic_slice.129
  674.3 1.3 dynamic_slice.130
  677.6 1.0 fusion.60
  678.7 1.3 dynamic_slice.129
  682.0 1.3 dynamic_slice.130
  685.4 1.0 fusion.60
  686.4 1.3 dynamic_slice.129
  689.8 1.3 dynamic_slice.130
  693.1 1.0 fusion.60
  694.2 1.3 dynamic_slice.129
  697.5 1.3 dynamic_slice.130
  700.9 1.0 fusion.60
  701.9 1.3 dynamic_slice.129
  705.3 1.3 dynamic_slice.130
  708.6 1.0 fusion.60
  709.7 1.3 dynamic_slice.129
  713.0 1.3 dynamic_slice.130
  716.4 1.0 fusion.60
  717.4 1.3 dynamic_slice.129
  720.8 1.3 dynamic_slice.130
  724.1 1.0 fusion.60
  725.2 1.3 dynamic_slice.129
  728.5 1.3 dynamic_slice.130
  731.8 1.0 fusion.60
  732.9 0.0 copy-start.5
  732.9 0.7 copy-done.5
  733.6 0.0 all-reduce.9.cloned.1.call-update
  733.6 0.0 all-gather.8.cloned.1.call-start
  733.7 325.9 %all-reduce.9.cloned.1.call-done = f32[8,128,64]{1,2,0:T(8,128)} async-done(((f32[8,128,64]{1,2,0:T(8,128)}), f32[8,128,64]{1,2,0:T(8,128)}) %all-reduce.9.cloned.1.call-update) | async-done | bytes 262160 | tf_op jit(solution)/shard_map/psum | solution.py:42
  1059.6 2.8 fusion.29
  1062.4 0.0 all-gather.8.cloned.1.call-update
  1062.4 0.0 all-reduce.11.cloned.1.call-start
  1063.1 45.4 %all-gather.8.cloned.1.call-done = f32[128,128,64]{1,2,0:T(8,128)} async-done(((f32[8,128,64]{1,2,0:T(8,128)}), f32[128,128,64]{1,2,0:T(8,128)}) %all-gather.8.cloned.1.call-update) | async-done | bytes 4194320 | tf_op jit(solution)/shard_map/all_gather | solution.py:48
  1108.6 0.7 copy-done.2
  1109.2 0.0 all-reduce.11.cloned.1.call-update
  1109.3 385.2 %all-reduce.11.cloned.1.call-done = f32[8,128,64]{1,2,0:T(8,128)} async-done(((f32[8,128,64]{1,2,0:T(8,128)}), f32[8,128,64]{1,2,0:T(8,128)}) %all-reduce.11.cloned.1.call-update) | async-done | bytes 262160 | tf_op jit(solution)/shard_map/psum | solution.py:42
  1494.4 2.9 fusion.28
  (18 shorter events, 0.2 us)
Async XLA Ops:
  6.5 160.8 %copy-start = (f32[8,128,128]{2,1,0:T(8,128)S(1)}, f32[8,128,128]{2,1,0:T(8,128)}, u32[]{:S(2)}) copy-start(f32[8,128,128]{2,1,0:T(8,128)} %param.16) | copy-start | bytes 1572868
  6.5 607.6 %copy-start.1 = (f32[8,128,64]{1,2,0:T(8,128)S(1)}, f32[8,128,64]{1,2,0:T(8,128)}, u32[]{:S(2)}) copy-start(f32[8,128,64]{1,2,0:T(8,128)} %param.15) | copy-start | bytes 786436
  6.5 160.8 %all-reduce.5.cloned.1.call-start = ((), (), s32[]{:S(2)}) async-start(), calls=%async_computation | async-start | bytes 524288 | tf_op jit(solution)/shard_map/psum | solution.py:42
  9.3 0.7 copy-start.3
  10.0 206.4 %all-gather.4.cloned.1.call-start = ((), (), s32[]{:S(2)}) async-start(), calls=%async_computation.1 | async-start | bytes 4456448 | tf_op jit(solution)/shard_map/all_gather | solution.py:48
  170.3 443.9 %all-reduce.7.cloned.1.call-start = ((), (), s32[]{:S(2)}) async-start(), calls=%async_computation.2 | async-start | bytes 524288 | tf_op jit(solution)/shard_map/psum | solution.py:42
  216.4 0.7 copy-start.4
  217.1 446.0 %all-gather.6.cloned.1.call-start = ((), (), s32[]{:S(2)}) async-start(), calls=%async_computation.3 | async-start | bytes 4456448 | tf_op jit(solution)/shard_map/all_gather | solution.py:48
  617.0 442.5 %all-reduce.9.cloned.1.call-start = ((), (), s32[]{:S(2)}) async-start(), calls=%async_computation.4 | async-start | bytes 524288 | tf_op jit(solution)/shard_map/psum | solution.py:42
  732.9 0.7 copy-start.5
  733.6 374.9 %all-gather.8.cloned.1.call-start = ((), (), s32[]{:S(2)}) async-start(), calls=%async_computation.5 | async-start | bytes 4456448 | tf_op jit(solution)/shard_map/all_gather | solution.py:48
  1062.4 432.1 %all-reduce.11.cloned.1.call-start = ((), (), s32[]{:S(2)}) async-start(), calls=%async_computation.6 | async-start | bytes 524288 | tf_op jit(solution)/shard_map/psum | solution.py:42
  1108.6 0.7 copy-start.2
Sparse Core Ops, SparseCore 0:
  10.8 156.5 all-reduce.4
  170.4 45.9 all-gather.3
  219.8 394.2 all-reduce.6
  617.2 45.9 all-gather.5
  733.7 325.8 all-reduce.8
  1062.5 45.9 all-gather.7
  1112.0 382.4 all-reduce.10
where the time goes:
time: 1510 us; the launch traced here: 1500 us
  waiting for transfers between devices  1400 us (93%)
  loops' own time  36.8 us (2%)
  local copies, waits for them, and re-layouts  27.8 us (2%)
  matrix products  20.6 us (1%)
  between operations  16.9 us (1%)
    psum x4, waiting for transfers between devices, body(): summed = lax.psum(partial_value, 'blk')  1270 us
    all_gather x3, waiting for transfers between devices, body(): solved_all = lax.all_gather(own_solution, 'leaf', axis=0, tiled=True)  136 us
    another operation x4, loops' own time, accumulate(): lax.fori_loop(0, trip_count, add_tile, jnp.zeros(partial_shape, jnp.float...  36.8 us
  transfers between devices with their start and end apart: 7, of which 7 were waited for; matrix products, arithmetic and copies ran while one was open for 0% of the time, Pallas kernels for 0%

commit v1 on v0

v1 whole, which is shorter than its diff:
```python
import functools

import jax
import jax.numpy as jnp
from jax import lax
from jax.experimental import pallas as pl
from jax.experimental.pallas import tpu as pltpu
from jax.sharding import PartitionSpec as P

LEVELS = 4
MESH = pl.DeviceIdType.MESH
F32 = jnp.float32
BF16 = jnp.bfloat16


def split(value):
    high = value.astype(BF16)
    return high, (value - high.astype(F32)).astype(BF16)


def kernel(
    cap, nl, nz, nx, slots, quarter, width,
    level_ref, rows_ref, cols_ref, count_ref, rhs_hbm, dinv_hbm, tiles_hbm,
    out_ref,
    tiles, dinv, rhs, rhs_t, weights, prods, part, from_x, to_z, from_z, piece, leaf0, leaf1, leaf2, gather0, gather1, gather2,
    final, mine, rank, names, slot_node, slot_level,
    local_sems, leaf_send, leaf_recv, rsx_send, rsx_recv, rsz_send, rsz_recv, agz_send, agz_recv, agx_send, agx_recv,
    core_send, core_recv,
):
    half = quarter // 2
    leaf, blk = lax.axis_index("leaf"), lax.axis_index("blk")
    core = lax.rem(leaf, 2)
    z, x = lax.div(blk, nx), lax.rem(blk, nx)
    gathers = (gather0, gather1, gather2)
    from_leaf = (leaf0, leaf1, leaf2)

    def z_peer(k):
        return lax.rem(z + k, nz)

    def x_peer(k):
        return lax.rem(x + k, nx)

    def at_z(k):
        return (leaf, z_peer(k) * nx + x)

    def at_x(k):
        return (leaf, z * nx + x_peer(k))

    def at_leaf(k):
        return (lax.rem(leaf + k, nl), blk)

    sibling = (leaf + 1 - 2 * core, blk)

    copies = [
        pltpu.make_async_copy(dinv_hbm.at[z], dinv, local_sems.at[0]),
        pltpu.make_async_copy(rhs_hbm.at[z], rhs, local_sems.at[1]),
        pltpu.make_async_copy(tiles_hbm, tiles, local_sems.at[2]),
    ]
    for copy in copies:
        copy.start()

    barrier = pltpu.get_barrier_semaphore()
    partners = [at_leaf(k) for k in range(1, nl)] + [at_z(k) for k in range(1, nz)] + [at_x(k) for k in range(1, nx)]
    for partner in partners:
        pl.semaphore_signal(barrier, inc=1, device_id=partner, device_id_type=MESH)

    for node in range(nl):
        at = jnp.int32(0)
        for other in range(node):
            at = at + jnp.where(level_ref[other] == level_ref[node], 1, 0)
        rank[node] = at
    for level in range(LEVELS - 1):
        for j in range(1 if level == 0 else cap):
            name = jnp.int32(0)
            for node in range(nl):
                name = name + jnp.where((level_ref[node] == level) & (rank[node] == j), node, 0)
            names[level * cap + j] = name

    def read_slot(s, _):
        node = lax.div(rows_ref[0, 0, s], nz)
        slot_node[s] = jnp.minimum(rank[node], cap - 1)
        slot_level[s] = jnp.where(s < count_ref[0, 0], level_ref[node], -1)
        return 0

    lax.fori_loop(0, slots, read_slot, 0)
    my_level = level_ref[leaf]

    copies[0].wait()
    copies[1].wait()
    rhs_t[...] = rhs[...].T
    own_rhs = rhs_t[pl.ds(pl.multiple_of(x * quarter, 8), quarter), :]

    def solve(summed):
        return lax.dot_general(
            own_rhs - summed, dinv[...], (((1,), (1,)), ((), ())),
            precision=lax.Precision.HIGHEST, preferred_element_type=F32,
        )

    piece[0] = solve(jnp.zeros((quarter, width), F32))
    mine[...] = piece[0]
    pl.semaphore_wait(barrier, len(partners))

    def wait_recv(ref, sem):
        pltpu.make_async_copy(ref, ref, sem).wait()

    def send(src, dst, send_sem, recv_sem, device):
        pltpu.make_async_remote_copy(
            src_ref=src, dst_ref=dst, send_sem=send_sem, recv_sem=recv_sem, device_id=device, device_id_type=MESH
        ).start()

    def leaf_start(level):
        for k in range(1, nl):
            peer = at_leaf(k)
            rows = pl.ds(pl.multiple_of(lax.rem(peer[0], 2) * half, 8), half)
            send(piece.at[level, rows], from_leaf[level].at[leaf], leaf_send.at[level], leaf_recv.at[level], peer)
        from_leaf[level][leaf] = piece[level, pl.ds(pl.multiple_of(core * half, 8), half), :]

    def broadcast(level):
        box = gathers[level]
        wait_recv(from_leaf[level].at[pl.ds(0, nl - 1)], leaf_recv.at[level])
        for j in range(1 if level == 0 else cap):
            box[core, x, z, j] = from_leaf[level][names[level * cap + j]]
        own = box.at[core, x, z]
        for k in range(1, nz):
            send(own, own, agz_send.at[level], agz_recv.at[level], at_z(k))
        wait_recv(box.at[core, x, pl.ds(0, nz - 1)], agz_recv.at[level])
        line = box.at[core, x]
        for k in range(1, nx):
            send(line, line, agx_send.at[level], agx_recv.at[level, k - 1], at_x(k))
        send(line, line, core_send.at[level], core_recv.at[level], sibling)
        for k in range(1, nx):
            wait_recv(line, agx_recv.at[level, k - 1])
            got = box.at[core, lax.rem(x + nx - k, nx)]
            send(got, got, core_send.at[level], core_recv.at[level], sibling)
        wait_recv(box.at[core], core_recv.at[level])

    def products(level):
        box = gathers[level - 1]

        def one(s, _):
            node = slot_node[s] if level > 1 else 0
            at = lax.rem(rows_ref[0, 0, s], nz)
            panel = jnp.concatenate([box[h, q, at, node] for q in range(nx) for h in range(2)], axis=0)
            high, low = split(panel)
            both = jnp.concatenate([high, low], axis=0)
            got = jnp.dot(both, weights[s], preferred_element_type=F32)
            n = nx * quarter
            prods[s] = (got[:n, width:] + got[n:, :width]) + got[:n, :width]
            return 0

        lax.fori_loop(0, slots, one, 0, unroll=4)

        def column(c, _):
            total = jnp.zeros((nx * quarter, width), F32)
            for s in range(slots):
                key = jnp.where(slot_level[s] == level - 1, cols_ref[0, 0, s], -1)
                total = total + jnp.where(key == c, 1.0, 0.0).astype(F32) * prods[s]
            for q in range(nx):
                mass = total[q * quarter : (q + 1) * quarter]
                part[q, c] = mass if level == 1 else part[q, c] + mass
            return 0

        lax.fori_loop(0, nz, column, 0)

    def reduce(level):
        at = level - 1
        for k in range(1, nx):
            send(part.at[x_peer(k)], from_x.at[at, k - 1], rsx_send.at[at], rsx_recv.at[at], at_x(k))
        wait_recv(from_x.at[at], rsx_recv.at[at])
        total = part[x]
        for k in range(nx - 1):
            total = total + from_x[at, k]
        to_z[at] = total
        for k in range(1, nz):
            send(to_z.at[at, z_peer(k)], from_z.at[at, k - 1], rsz_send.at[at], rsz_recv.at[at], at_z(k))
        wait_recv(from_z.at[at], rsz_recv.at[at])
        total = to_z[at, z]
        for k in range(nz - 1):
            total = total + from_z[at, k]
        return total

    def drain_part(level):
        wait_recv(from_x.at[level - 1], rsx_send.at[level - 1])

    leaf_start(0)
    copies[2].wait()

    def prepare(s, _):
        high, low = split(tiles[s])
        weights[s, :, :width] = high
        weights[s, :, width:] = low
        return 0

    lax.fori_loop(0, slots, prepare, 0, unroll=2)
    broadcast(0)
    for level in range(1, LEVELS):
        if level > 1:
            drain_part(level - 1)
        products(level)
        solved = solve(reduce(level))
        piece[level] = solved
        keep = jnp.where(my_level == level, 1.0, 0.0).astype(F32)
        mine[...] = keep * solved + (1.0 - keep) * mine[...]
        if level + 1 < LEVELS:
            leaf_start(level)
            broadcast(level)

    last = LEVELS - 1
    final[x, z] = mine[...]
    own = final.at[x, z]
    for k in range(1, nz):
        send(own, own, agz_send.at[last], agz_recv.at[last], at_z(k))
    wait_recv(final.at[x, pl.ds(0, nz - 1)], agz_recv.at[last])
    line = final.at[x]
    for k in range(1, nx):
        send(line, line, agx_send.at[last], agx_recv.at[last, k - 1], at_x(k))
    for k in range(1, nx):
        wait_recv(line, agx_recv.at[last, k - 1])
    for q in range(nx):
        out_ref[:, pl.ds(q * quarter, quarter), :] = final[q]

    drain_part(last)
    for at in range(LEVELS - 1):
        wait_recv(from_z.at[at], rsz_send.at[at])
        wait_recv(from_leaf[at].at[pl.ds(0, nl - 1)], leaf_send.at[at])
        box = gathers[at]
        wait_recv(box.at[0, 0, pl.ds(0, nz - 1)], agz_send.at[at])
        wait_recv(box.at[0, pl.ds(0, nx - 1)], agx_send.at[at])
        wait_recv(box.at[0], core_send.at[at])
    wait_recv(final.at[0, pl.ds(0, nz - 1)], agz_send.at[last])
    wait_recv(final.at[pl.ds(0, nx - 1)], agx_send.at[last])


def body(cap, adjoint_rhs, diag_inverse, blocks, block_rows, block_cols, block_count, node_level):
    per_node, width, columns = adjoint_rhs.shape
    slots = blocks.shape[2]
    nl, nb = lax.axis_size("leaf"), lax.axis_size("blk")
    nz = per_node
    nx = nb // nz
    quarter = columns // nx
    half = quarter // 2
    last = LEVELS - 1
    dma = pltpu.SemaphoreType.DMA
    smem = pl.BlockSpec(memory_space=pltpu.SMEM)
    hbm = pl.BlockSpec(memory_space=pl.ANY)
    vmem = pltpu.VMEM
    solved = pl.pallas_call(
        functools.partial(kernel, cap, nl, nz, nx, slots, quarter, width),
        out_shape=jax.ShapeDtypeStruct((per_node, columns, width), F32),
        in_specs=[smem] * 4 + [hbm] * 3,
        out_specs=pl.BlockSpec(memory_space=pltpu.VMEM),
        scratch_shapes=[
            vmem((slots, width, width), F32),
            vmem((width, width), F32),
            vmem((width, columns), F32),
            vmem((columns, width), F32),
            vmem((slots, width, 2 * width), BF16),
            vmem((slots, columns, width), F32),
            vmem((nx, nz, quarter, width), F32),
            vmem((last, nx - 1, nz, quarter, width), F32),
            vmem((last, nz, quarter, width), F32),
            vmem((last, nz - 1, quarter, width), F32),
            vmem((LEVELS, quarter, width), F32),
            vmem((nl, half, width), F32),
            vmem((nl, half, width), F32),
            vmem((nl, half, width), F32),
            vmem((2, nx, nz, 1, half, width), F32),
            vmem((2, nx, nz, cap, half, width), F32),
            vmem((2, nx, nz, cap, half, width), F32),
            vmem((nx, nz, quarter, width), F32),
            vmem((quarter, width), F32),
            pltpu.SMEM((nl,), jnp.int32),
            pltpu.SMEM((last * cap,), jnp.int32),
            pltpu.SMEM((slots,), jnp.int32),
            pltpu.SMEM((slots,), jnp.int32),
            dma((3,)),
            dma((last,)),
            dma((last,)),
            dma((last,)),
            dma((last,)),
            dma((last,)),
            dma((last,)),
            dma((LEVELS,)),
            dma((LEVELS,)),
            dma((LEVELS,)),
            dma((LEVELS, nx - 1)),
            dma((last,)),
            dma((last,)),
        ],
        compiler_params=pltpu.CompilerParams(
            collective_id=0, has_side_effects=True, vmem_limit_bytes=48 * 1024 * 1024
        ),
        name="tree_solve",
    )(
        node_level, block_rows.reshape(1, 1, slots), block_cols.reshape(1, 1, slots), block_count,
        adjoint_rhs, diag_inverse, blocks.reshape(slots, width, width),
    )
    return jnp.swapaxes(solved, 1, 2)


def solution(mesh):
    in_specs = (
        P("leaf", None, None),
        P("leaf", None, None),
        P("leaf", "blk", None, None, None),
        P("leaf", "blk", None),
        P("leaf", "blk", None),
        P("leaf", "blk"),
        P(),
    )
    out_specs = P("leaf", None, None)
    cap = mesh.shape["leaf"] - 3
    return jax.shard_map(
        functools.partial(body, cap), mesh=mesh, in_specs=in_specs, out_specs=out_specs, check_vma=False
    )
```

time: 1510 us -> 164 us (0.11)
  waiting for transfers between devices: 1400 us -> 0 us
  Pallas kernels: 0 us -> 157 us
  loops' own time: 36.8 us -> 0 us
  local copies, waits for them, and re-layouts: 27.8 us -> 6.45 us
  matrix products: 20.6 us -> 0 us
  between operations: 16.9 us -> 0.68 us
    psum x4 -> x0, waiting for transfers between devices: 1270 us -> none  [body(): summed = lax.psum(partial_value, 'blk')]
    pallas_call x0 -> x1, Pallas kernels: none -> 157 us  [body(): pl.pallas_call(functools.partial(kernel, cap, nl, nz, nx, slots, quarter,...]
    all_gather x3 -> x0, waiting for transfers between devices: 136 us -> none  [body(): solved_all = lax.all_gather(own_solution, 'leaf', axis=0, tiled=True)]
    another operation x4 -> x0, loops' own time: 36.8 us -> none  [accumulate(): lax.fori_loop(0, trip_count, add_tile, jnp.zeros(partial_shape, jnp.float...]
    dynamic_slice x28 -> x0, local copies, waits for them, and re-layouts: 24.9 us -> none  [the longest x9 11.8 us: add_tile(): row_at = lax.dynamic_index_in_dim(row_ids, slot_at, 0, keepdims=False)]
    dot_general x13 -> x0, matrix products: 20.6 us -> none  [the longest x4 11.3 us: body(): jnp.einsum('cij,cjk->cik', diag_inverse, adjoint_rhs - summed, precision=...]
  transfers between devices with their start and end apart: 7 -> 0, of which waited for: 7 -> 0; matrix products, arithmetic and copies ran while one was open for 0% -> 0% of each run, Pallas kernels for 0% -> 0%
where the time goes in v1:
time: 164 us
  Pallas kernels  157 us (96%)
  local copies, waits for them, and re-layouts  6.45 us (4%)
    pallas_call x1, Pallas kernels, body(): pl.pallas_call(functools.partial(kernel, cap, nl, nz, nx, slots, quarter,...  157 us
    unnamed x12, local copies, waits for them, and re-layouts  6.45 us

profile of v1, /device:TPU:1, one launch (start us, length us, event | category | flops | bytes accessed | tf_op | source)
XLA Modules:
  0.0 163.9 jit_solution(15345338439510572656)
XLA Ops:
  0.7 1.1 copy.8.rhs_hbm
  1.8 0.0 copy-start
  1.8 1.6 copy-done
  3.4 0.0 copy-start.1
  3.4 1.0 copy-done.1
  4.4 0.0 copy-start.2
  4.4 0.7 copy-done.2
  5.1 0.0 copy-start.3
  5.1 0.7 copy-done.3
  5.8 0.0 copy-start.4
  5.8 0.7 copy-done.4
  6.4 156.7 %tree_solve.1 = f32[8,64,128]{2,1,0:T(8,128)S(1)} custom-call(s32[16]{0:T(128)S(1)} %copy-done.2, s32[1,1,32]{2,1,0:T(1,128)S(1)} %copy-done.3, s32[1,1,32]{2,1,0:T(1,128)S(1)} %copy-done.4, s32[1,1]{1,0:T(1,128)S(6)} %copy.10.count_ref, f32[8,128,64]{2,1,0:T(8,128)S(1)} %copy.8.rhs_hbm, f32[8,128,128]{2,1,0:T(8,128)S(1)} %copy-done.1, ...), custom_call_target="tpu_custom_call" | custom-call | tf_op jit(solution)/shard_map/tree_solve/pallas_call | solution.py:247
  163.2 0.7 copy.11
Async XLA Ops:
  1.8 1.6 copy-start
  3.4 1.0 copy-start.1
  4.4 0.7 copy-start.2
  5.1 0.7 copy-start.3
  5.8 0.7 copy-start.4

commit v2 on v1

v2 whole, which is shorter than its diff:
```python
import functools

import jax
import jax.numpy as jnp
from jax import lax
from jax.experimental import pallas as pl
from jax.experimental.pallas import tpu as pltpu
from jax.sharding import PartitionSpec as P

LEVELS = 4
VMEM_LIMIT = 60 * 1024 * 1024
MESH = pl.DeviceIdType.MESH
F32 = jnp.float32
BF16 = jnp.bfloat16


def split(value):
    high = value.astype(BF16)
    return high, (value - high.astype(F32)).astype(BF16)


def kernel(
    cap, nl, nz, nx, slots, quarter, width,
    level_hbm, rows_hbm, cols_hbm, count_hbm, rhs_hbm, dinv_hbm, tiles_hbm,
    out_ref, flag_ref,
    level_ref, rows_ref, cols_ref, count_ref,
    tiles, dinv, own_rhs, weights, prods, part, from_x, to_z, from_z, piece, leaf0, leaf1, leaf2, gather0, gather1, gather2,
    final, mine, need, need_z, need_x, flags, rank, names, slot_node, slot_level,
    local_sems, leaf_send, leaf_recv, rsx_send, rsx_recv, rsz_send, rsz_recv, agz_send, agz_recv, agx_send, agx_recv,
    core_send, core_recv, need_send, need_recv,
):
    fast = cap == 0
    half = quarter // 2
    leaf, blk = lax.axis_index("leaf"), lax.axis_index("blk")
    core = lax.rem(leaf, 2)
    z, x = lax.div(blk, nx), lax.rem(blk, nx)
    gathers = (gather0, gather1, gather2)
    from_leaf = (leaf0, leaf1, leaf2)

    def z_peer(k):
        return lax.rem(z + k, nz)

    def x_peer(k):
        return lax.rem(x + k, nx)

    def at_z(k):
        return (leaf, z_peer(k) * nx + x)

    def at_x(k):
        return (leaf, z * nx + x_peer(k))

    def at_leaf(k):
        return (lax.rem(leaf + k, nl), blk)

    sibling = (leaf + 1 - 2 * core, blk)

    barrier = pltpu.get_barrier_semaphore()
    partners = [at_leaf(k) for k in range(1, nl)] + [at_z(k) for k in range(1, nz)] + [at_x(k) for k in range(1, nx)]
    for partner in partners:
        pl.semaphore_signal(barrier, inc=1, device_id=partner, device_id_type=MESH)

    copies = [
        pltpu.make_async_copy(dinv_hbm.at[z], dinv, local_sems.at[0]),
        pltpu.make_async_copy(
            rhs_hbm.at[z, pl.ds(pl.multiple_of(x * quarter, 8), quarter)], own_rhs, local_sems.at[1]
        ),
        pltpu.make_async_copy(level_hbm, level_ref, local_sems.at[2]),
        pltpu.make_async_copy(rows_hbm, rows_ref, local_sems.at[3]),
        pltpu.make_async_copy(cols_hbm, cols_ref, local_sems.at[4]),
        pltpu.make_async_copy(count_hbm, count_ref, local_sems.at[5]),
        pltpu.make_async_copy(tiles_hbm, tiles, local_sems.at[6]),
    ]
    for copy in copies:
        copy.start()

    def solve(summed):
        return lax.dot_general(
            own_rhs[...] - summed, dinv[...], (((1,), (1,)), ((), ())),
            precision=lax.Precision.HIGHEST, preferred_element_type=F32,
        )

    copies[0].wait()
    copies[1].wait()
    piece[0] = solve(jnp.zeros((quarter, width), F32))
    mine[...] = piece[0]
    for copy in copies[2:6]:
        copy.wait()

    if fast:
        root = jnp.int32(0)
        for node in range(nl):
            root = jnp.maximum(root, jnp.where(level_ref[node] == 0, node, 0))
        names[0] = root
    else:
        for node in range(nl):
            at = jnp.int32(0)
            for other in range(node):
                at = at + jnp.where(level_ref[other] == level_ref[node], 1, 0)
            rank[node] = at
        for level in range(LEVELS - 1):
            for j in range(1 if level == 0 else cap):
                name = jnp.int32(0)
                for node in range(nl):
                    name = name + jnp.where((level_ref[node] == level) & (rank[node] == j), node, 0)
                names[level * cap + j] = name

    def read_slot(s, seen):
        node = lax.div(rows_ref[0, 0, s], nz)
        level = jnp.where(s < count_ref[0, 0], level_ref[node], -1)
        slot_level[s] = level
        if not fast:
            slot_node[s] = jnp.minimum(rank[node], cap - 1)
        top1, low1, top2, low2 = seen
        return (
            jnp.maximum(top1, jnp.where(level == 1, node, -1)),
            jnp.maximum(low1, jnp.where(level == 1, -node, -nl)),
            jnp.maximum(top2, jnp.where(level == 2, node, -1)),
            jnp.maximum(low2, jnp.where(level == 2, -node, -nl)),
        )

    first = (jnp.int32(-1), jnp.int32(-nl), jnp.int32(-1), jnp.int32(-nl))
    seen = lax.fori_loop(0, slots, read_slot, first)
    my_level = level_ref[leaf]
    pl.semaphore_wait(barrier, len(partners))

    def wait_bytes(ref, sem):
        pltpu.make_async_copy(ref, ref, sem).wait()

    drains = []

    def send(src, dst, send_sem, recv_sem, device):
        pltpu.make_async_remote_copy(
            src_ref=src, dst_ref=dst, send_sem=send_sem, recv_sem=recv_sem, device_id=device, device_id_type=MESH
        ).start()

    def halves(level):
        return level == 0 or not fast

    def leaf_start(level):
        for k in range(1, nl):
            peer = at_leaf(k)
            rows = pl.ds(pl.multiple_of(lax.rem(peer[0], 2) * half, 8), half)
            src = piece.at[level, rows] if halves(level) else piece.at[level]
            send(src, from_leaf[level].at[leaf], leaf_send.at[level], leaf_recv.at[level], peer)
        if halves(level):
            from_leaf[level][leaf] = piece[level, pl.ds(pl.multiple_of(core * half, 8), half), :]
        else:
            from_leaf[level][leaf] = piece[level]
        drains.append((from_leaf[level].at[pl.ds(0, nl - 1)], leaf_send.at[level]))

    def broadcast_listed(level):
        box = gathers[level]
        wait_bytes(from_leaf[level].at[pl.ds(0, nl - 1)], leaf_recv.at[level])
        for j in range(1 if level == 0 else cap):
            box[core, x, z, j] = from_leaf[level][names[level * cap + j]]
        own = box.at[core, x, z]
        for k in range(1, nz):
            send(own, own, agz_send.at[level], agz_recv.at[level], at_z(k))
        if level == 0 and fast:
            need_across()
        wait_bytes(box.at[core, x, pl.ds(0, nz - 1)], agz_recv.at[level])
        line = box.at[core, x]
        for k in range(1, nx):
            send(line, line, agx_send.at[level], agx_recv.at[level, k - 1], at_x(k))
        send(line, line, core_send.at[level], core_recv.at[level], sibling)
        for k in range(1, nx):
            wait_bytes(line, agx_recv.at[level, k - 1])
            got = box.at[core, lax.rem(x + nx - k, nx)]
            send(got, got, core_send.at[level], core_recv.at[level], sibling)
        wait_bytes(box.at[core], core_recv.at[level])
        drains.append((box.at[0, 0, pl.ds(0, nz - 1)], agz_send.at[level]))
        drains.append((box.at[0, pl.ds(0, nx - 1)], agx_send.at[level]))
        drains.append((box.at[0], core_send.at[level]))

    def gather_plane(box, value, level):
        box[x, z] = value
        own = box.at[x, z]
        for k in range(1, nz):
            send(own, own, agz_send.at[level], agz_recv.at[level], at_z(k))
        wait_bytes(box.at[x, pl.ds(0, nz - 1)], agz_recv.at[level])
        line = box.at[x]
        for k in range(1, nx):
            send(line, line, agx_send.at[level], agx_recv.at[level, 0], at_x(k))
        wait_bytes(box.at[pl.ds(0, nx - 1)], agx_recv.at[level, 0])
        drains.append((box.at[0, pl.ds(0, nz - 1)], agz_send.at[level]))
        drains.append((box.at[pl.ds(0, nx - 1)], agx_send.at[level]))

    def broadcast(level):
        if halves(level):
            broadcast_listed(level)
            return
        wait_bytes(from_leaf[level].at[pl.ds(0, nl - 1)], leaf_recv.at[level])
        wanted = need[2 * level - 2 : 2 * level - 1, :]
        chosen = jnp.zeros((quarter, width), F32)
        for node in range(nl):
            chosen = jnp.where(wanted == float(node), from_leaf[level][node], chosen)
        gather_plane(gathers[level], chosen, level)

    def need_start():
        at = lax.broadcasted_iota(jnp.int32, (8, width), 0)
        tile = jnp.full((8, width), -float(nl), F32)
        for i, value in enumerate(seen):
            tile = jnp.where(at == i, value.astype(F32), tile)
        need[...] = tile
        for k in range(1, nz):
            send(need, need_z.at[k - 1], need_send.at[0], need_recv.at[0], at_z(k))

    def need_across():
        wait_bytes(need_z, need_recv.at[0])
        wait_bytes(need_z, need_send.at[0])
        tile = need[...]
        for k in range(nz - 1):
            tile = jnp.maximum(tile, need_z[k])
        need[...] = tile
        for k in range(1, nx):
            send(need, need_x.at[k - 1], need_send.at[1], need_recv.at[1], at_x(k))

    def need_end():
        wait_bytes(need_x, need_recv.at[1])
        wait_bytes(need_x, need_send.at[1])
        tile = need[...]
        for k in range(nx - 1):
            tile = jnp.maximum(tile, need_x[k])
        need[...] = tile
        several = (tile[0:1] + tile[1:2] > 0.0) | (tile[2:3] + tile[3:4] > 0.0)
        flags[leaf] = jnp.where(jnp.broadcast_to(several, (8, width)), 1.0, 0.0).astype(F32)
        for k in range(1, nl):
            send(flags.at[leaf], flags.at[leaf], need_send.at[2], need_recv.at[2], at_leaf(k))
        drains.append((flags.at[pl.ds(0, nl - 1)], need_send.at[2]))

    def products(level):
        box = gathers[level - 1]

        def one(s, _):
            at = lax.rem(rows_ref[0, 0, s], nz)
            if halves(level - 1):
                node = slot_node[s] if level > 1 else 0
                panel = jnp.concatenate([box[h, q, at, node] for q in range(nx) for h in range(2)], axis=0)
            else:
                panel = jnp.concatenate([box[q, at] for q in range(nx)], axis=0)
            high, low = split(panel)
            both = jnp.concatenate([high, low], axis=0)
            got = jnp.dot(both, weights[s], preferred_element_type=F32)
            n = nx * quarter
            prods[s] = (got[:n, width:] + got[n:, :width]) + got[:n, :width]
            return 0

        lax.fori_loop(0, slots, one, 0, unroll=4)

        def column(c, _):
            total = jnp.zeros((nx * quarter, width), F32)
            for s in range(slots):
                key = jnp.where(slot_level[s] == level - 1, cols_ref[0, 0, s], -1)
                total = total + jnp.where(key == c, 1.0, 0.0).astype(F32) * prods[s]
            for q in range(nx):
                mass = total[q * quarter : (q + 1) * quarter]
                part[q, c] = mass if level == 1 else part[q, c] + mass
            return 0

        lax.fori_loop(0, nz, column, 0)

    def reduce(level):
        at = level - 1
        for k in range(1, nx):
            send(part.at[x_peer(k)], from_x.at[at, k - 1], rsx_send.at[at], rsx_recv.at[at], at_x(k))
        if level == 1 and fast:
            need_end()
        wait_bytes(from_x.at[at], rsx_recv.at[at])
        total = part[x]
        for k in range(nx - 1):
            total = total + from_x[at, k]
        to_z[at] = total
        for k in range(1, nz):
            send(to_z.at[at, z_peer(k)], from_z.at[at, k - 1], rsz_send.at[at], rsz_recv.at[at], at_z(k))
        wait_bytes(from_z.at[at], rsz_recv.at[at])
        total = to_z[at, z]
        for k in range(nz - 1):
            total = total + from_z[at, k]
        drains.append((from_z.at[at], rsz_send.at[at]))
        return total

    def drain_part(level):
        wait_bytes(from_x.at[level - 1], rsx_send.at[level - 1])

    leaf_start(0)
    if fast:
        need_start()
    copies[6].wait()

    def prepare(s, _):
        high, low = split(tiles[s])
        weights[s, :, :width] = high
        weights[s, :, width:] = low
        return 0

    lax.fori_loop(0, slots, prepare, 0, unroll=2)
    broadcast(0)
    for level in range(1, LEVELS):
        if level > 1:
            drain_part(level - 1)
        products(level)
        solved = solve(reduce(level))
        piece[level] = solved
        keep = jnp.where(my_level == level, 1.0, 0.0).astype(F32)
        mine[...] = keep * solved + (1.0 - keep) * mine[...]
        if level + 1 < LEVELS:
            leaf_start(level)
            broadcast(level)

    gather_plane(final, mine[...], LEVELS - 1)
    for q in range(nx):
        out_ref[:, pl.ds(q * quarter, quarter), :] = final[q]

    if fast:
        wait_bytes(flags.at[pl.ds(0, nl - 1)], need_recv.at[2])
        flag = flags[0]
        for node in range(1, nl):
            flag = jnp.maximum(flag, flags[node])
        flag_ref[...] = flag
    else:
        flag_ref[...] = jnp.zeros_like(flag_ref)
    drain_part(LEVELS - 1)
    for ref, sem in drains:
        wait_bytes(ref, sem)


def call(cap, rhs_t, diag_inverse, tiles, block_rows, block_cols, block_count, node_level):
    per_node, columns, width = rhs_t.shape
    slots = tiles.shape[0]
    nl, nb = lax.axis_size("leaf"), lax.axis_size("blk")
    nz = per_node
    nx = nb // nz
    quarter = columns // nx
    half = quarter // 2
    last = LEVELS - 1
    fast = cap == 0
    dma = pltpu.SemaphoreType.DMA
    hbm = pl.BlockSpec(memory_space=pltpu.HBM)
    vmem = pltpu.VMEM
    smem = pltpu.SMEM
    whole = pl.BlockSpec(memory_space=pltpu.VMEM)
    box = (nx, nz, quarter, width) if fast else (2, nx, nz, cap, half, width)
    side = (nl, quarter, width) if fast else (nl, half, width)
    return pl.pallas_call(
        functools.partial(kernel, cap, nl, nz, nx, slots, quarter, width),
        out_shape=(
            jax.ShapeDtypeStruct((per_node, columns, width), F32),
            jax.ShapeDtypeStruct((8, width), F32),
        ),
        in_specs=[hbm] * 7,
        out_specs=(whole, whole),
        scratch_shapes=[
            smem(node_level.shape, jnp.int32),
            smem(block_rows.shape, jnp.int32),
            smem(block_cols.shape, jnp.int32),
            smem(block_count.shape, jnp.int32),
            vmem((slots, width, width), F32),
            vmem((width, width), F32),
            vmem((quarter, width), F32),
            vmem((slots, width, 2 * width), BF16),
            vmem((slots, columns, width), F32),
            vmem((nx, nz, quarter, width), F32),
            vmem((last, nx - 1, nz, quarter, width), F32),
            vmem((last, nz, quarter, width), F32),
            vmem((last, nz - 1, quarter, width), F32),
            vmem((LEVELS, quarter, width), F32),
            vmem((nl, half, width), F32),
            vmem(side, F32),
            vmem(side, F32),
            vmem((2, nx, nz, 1, half, width), F32),
            vmem(box, F32),
            vmem(box, F32),
            vmem((nx, nz, quarter, width), F32),
            vmem((quarter, width), F32),
            vmem((8, width), F32),
            vmem((nz - 1, 8, width), F32),
            vmem((nx - 1, 8, width), F32),
            vmem((nl, 8, width), F32),
            smem((nl,), jnp.int32),
            smem((last * max(cap, 1),), jnp.int32),
            smem((slots,), jnp.int32),
            smem((slots,), jnp.int32),
            dma((7,)),
            dma((last,)),
            dma((last,)),
            dma((last,)),
            dma((last,)),
            dma((last,)),
            dma((last,)),
            dma((LEVELS,)),
            dma((LEVELS,)),
            dma((LEVELS,)),
            dma((LEVELS, nx - 1)),
            dma((last,)),
            dma((last,)),
            dma((3,)),
            dma((3,)),
        ],
        compiler_params=pltpu.CompilerParams(
            collective_id=0 if fast else 1, has_side_effects=True, vmem_limit_bytes=VMEM_LIMIT
        ),
        name="tree_solve" if fast else "tree_solve_listed",
    )(node_level, block_rows, block_cols, block_count, rhs_t, diag_inverse, tiles)


def body(adjoint_rhs, diag_inverse, blocks, block_rows, block_cols, block_count, node_level):
    args = (
        jnp.swapaxes(adjoint_rhs, 1, 2), diag_inverse, blocks.reshape(blocks.shape[2:]),
        block_rows, block_cols, block_count, node_level,
    )
    solved, flag = call(0, *args)
    cap = lax.axis_size("leaf") - 3
    solved = lax.cond(flag[0, 0] > 0.5, lambda: call(cap, *args)[0], lambda: solved)
    return jnp.swapaxes(solved, 1, 2)


def solution(mesh):
    in_specs = (
        P("leaf", None, None),
        P("leaf", None, None),
        P("leaf", "blk", None, None, None),
        P("leaf", "blk", None),
        P("leaf", "blk", None),
        P("leaf", "blk"),
        P(),
    )
    out_specs = P("leaf", None, None)
    return jax.shard_map(body, mesh=mesh, in_specs=in_specs, out_specs=out_specs, check_vma=False)
```

time: 164 us -> 113 us (0.69)
  the two profiles are of different devices: /device:TPU:1 before, /device:TPU:4 now
where the time goes in v2:
time: 113 us; the launch traced here: 112 us
  Pallas kernels  109 us (96%)
  local copies, waits for them, and re-layouts  1.91 us (2%)
  between operations  1.54 us (1%)
    pallas_call x1, Pallas kernels, call(): pl.pallas_call(functools.partial(kernel, cap, nl, nz, nx, slots, quarter,...  109 us

profile of v2, /device:TPU:4, one launch (start us, length us, event | category | flops | bytes accessed | tf_op | source)
XLA Modules:
  0.0 112.4 jit_solution(14952711636321811988)
XLA Ops:
  0.0 0.0 copy-start.3
  0.0 0.0 copy-start.5
  0.0 0.0 copy-start.4
  0.0 0.0 copy-start.1
  0.0 0.0 copy-start
  0.0 0.0 copy-start.2
  0.8 108.9 %tree_solve.1 = (f32[8,64,128]{2,1,0:T(8,128)S(1)}, f32[8,128]{1,0:T(8,128)}) custom-call(s32[16]{0:T(128)} %level_hbm.1, s32[1,1,32]{2,1,0:T(1,128)} %rows_hbm.1, s32[1,1,32]{2,1,0:T(1,128)} %cols_hbm.1, s32[1,1]{1,0:T(1,128)S(6)} %copy.11.count_hbm, f32[8,64,128]{2,1,0:T(8,128)} %bitcast.6, f32[8,128,128]{2,1,0:T(8,128)} %dinv_hbm.1, f32[32,128,128]{2,1,0:T(8,128)} %bitcast.4), custom_call_target="tpu_custom_call" | custom-call | tf_op jit(solution)/shard_map/tree_solve/pallas_call | solution.py:344
  109.8 1.2 %slice.3 = f32[1,1]{1,0:T(1,128)} slice(f32[8,128]{1,0:T(8,128)} %get-tuple-element.33), slice={[0:1], [0:1]} | slice | bytes 8 | tf_op jit(solution)/shard_map/slice | solution.py:413
  111.6 0.0 copy-done.3
  111.6 0.0 copy-done.5
  111.6 0.0 copy-done.4
  111.6 0.0 copy-done.1
  111.6 0.0 copy-done
  111.7 0.0 copy-done.2
  111.7 0.7 copy.12
  (1 shorter events, 0.0 us)
Async XLA Ops:
  0.0 111.6 %copy-start.3 = (s32[16]{0:T(128)S(1)}, s32[16]{0:T(128)}, u32[]{:S(2)}) copy-start(s32[16]{0:T(128)} %level_hbm.1) | copy-start | bytes 196
  0.0 111.6 %copy-start.5 = (s32[1,1,32]{2,1,0:T(1,128)S(1)}, s32[1,1,32]{2,1,0:T(1,128)}, u32[]{:S(2)}) copy-start(s32[1,1,32]{2,1,0:T(1,128)} %cols_hbm.1) | copy-start | bytes 388
  0.0 111.6 %copy-start.4 = (s32[1,1,32]{2,1,0:T(1,128)S(1)}, s32[1,1,32]{2,1,0:T(1,128)}, u32[]{:S(2)}) copy-start(s32[1,1,32]{2,1,0:T(1,128)} %rows_hbm.1) | copy-start | bytes 388
  0.0 111.6 %copy-start.1 = (f32[8,128,128]{2,1,0:T(8,128)S(1)}, f32[8,128,128]{2,1,0:T(8,128)}, u32[]{:S(2)}) copy-start(f32[8,128,128]{2,1,0:T(8,128)} %dinv_hbm.1) | copy-start | bytes 1572868
  0.0 111.6 %copy-start = (f32[1,1,32,128,128]{4,3,2,1,0:T(8,128)S(1)}, f32[1,1,32,128,128]{4,3,2,1,0:T(8,128)}, u32[]{:S(2)}) copy-start(f32[1,1,32,128,128]{4,3,2,1,0:T(8,128)} %param.11) | copy-start | bytes 6291460
  0.0 111.6 %copy-start.2 = (f32[8,128,64]{1,2,0:T(8,128)S(1)}, f32[8,128,64]{1,2,0:T(8,128)}, u32[]{:S(2)}) copy-start(f32[8,128,64]{1,2,0:T(8,128)} %param.9) | copy-start | bytes 786436

commit v3 on v2

--- a/solution.py
+++ b/solution.py
@@ -24,9 +24,9 @@
     level_hbm, rows_hbm, cols_hbm, count_hbm, rhs_hbm, dinv_hbm, tiles_hbm,
     out_ref, flag_ref,
     level_ref, rows_ref, cols_ref, count_ref,
-    tiles, dinv, own_rhs, weights, prods, part, from_x, to_z, from_z, piece, leaf0, leaf1, leaf2, gather0, gather1, gather2,
+    tiles, dinv, own_rhs, weights, prods, part, from_plane, piece, leaf0, leaf1, leaf2, gather0, gather1, gather2,
     final, mine, need, need_z, need_x, flags, rank, names, slot_node, slot_level,
-    local_sems, leaf_send, leaf_recv, rsx_send, rsx_recv, rsz_send, rsz_recv, agz_send, agz_recv, agx_send, agx_recv,
+    local_sems, leaf_send, leaf_recv, part_send, part_recv, agz_send, agz_recv, agx_send, agx_recv,
     core_send, core_recv, need_send, need_recv,
 ):
     fast = cap == 0
@@ -136,8 +136,10 @@
     def halves(level):
         return level == 0 or not fast
 
+    leaf_order = [nl // 2 + (-1) ** i * ((i + 1) // 2) for i in range(nl - 1)]
+
     def leaf_start(level):
-        for k in range(1, nl):
+        for k in leaf_order:
             peer = at_leaf(k)
             rows = pl.ds(pl.multiple_of(lax.rem(peer[0], 2) * half, 8), half)
             src = piece.at[level, rows] if halves(level) else piece.at[level]
@@ -148,16 +150,53 @@
             from_leaf[level][leaf] = piece[level]
         drains.append((from_leaf[level].at[pl.ds(0, nl - 1)], leaf_send.at[level]))
 
+    def far_first(i, n):
+        step = lax.div(i + 1, 2)
+        return jnp.where(lax.rem(i, 2) == 1, n // 2 - step, n // 2 + step)
+
+    def plane_loop(visit):
+        order = [nx // 2 + (-1) ** i * ((i + 1) // 2) for i in range(nx)]
+
+        def one(i, _):
+            dz = far_first(i, nz)
+            visit(dz, order)
+            return 0
+
+        lax.fori_loop(0, nz - 1, one, 0)
+        visit(0, [dx for dx in order if dx])
+
+    def send_all(own, box_at, send_sem, recv_sem):
+        def visit(dz, order):
+            for dx in order:
+                send(own, box_at, send_sem, recv_sem, (leaf, z_peer(dz) * nx + x_peer(dx)))
+
+        plane_loop(visit)
+
+    def gather_plane(box, level):
+        own = box.at[blk]
+        send_all(own, own, agz_send.at[level], agz_recv.at[level])
+        others = box.at[pl.ds(0, nz * nx - 1)]
+        wait_bytes(others, agz_recv.at[level])
+        drains.append((others, agz_send.at[level]))
+
+    def broadcast_root():
+        box = gather0
+        wait_bytes(leaf0.at[pl.ds(0, nl - 1)], leaf_recv.at[0])
+        need_across()
+        box[core, blk] = leaf0[names[0]]
+        side = box.at[core]
+        gather_plane(side, 0)
+        send(side, side, core_send.at[0], core_recv.at[0], sibling)
+        wait_bytes(side, core_recv.at[0])
+        drains.append((side, core_send.at[0]))
+
     def broadcast_listed(level):
         box = gathers[level]
-        wait_bytes(from_leaf[level].at[pl.ds(0, nl - 1)], leaf_recv.at[level])
-        for j in range(1 if level == 0 else cap):
+        for j in range(cap):
             box[core, x, z, j] = from_leaf[level][names[level * cap + j]]
         own = box.at[core, x, z]
         for k in range(1, nz):
             send(own, own, agz_send.at[level], agz_recv.at[level], at_z(k))
-        if level == 0 and fast:
-            need_across()
         wait_bytes(box.at[core, x, pl.ds(0, nz - 1)], agz_recv.at[level])
         line = box.at[core, x]
         for k in range(1, nx):
@@ -172,29 +211,17 @@
         drains.append((box.at[0, pl.ds(0, nx - 1)], agx_send.at[level]))
         drains.append((box.at[0], core_send.at[level]))
 
-    def gather_plane(box, value, level):
-        box[x, z] = value
-        own = box.at[x, z]
-        for k in range(1, nz):
-            send(own, own, agz_send.at[level], agz_recv.at[level], at_z(k))
-        wait_bytes(box.at[x, pl.ds(0, nz - 1)], agz_recv.at[level])
-        line = box.at[x]
-        for k in range(1, nx):
-            send(line, line, agx_send.at[level], agx_recv.at[level, 0], at_x(k))
-        wait_bytes(box.at[pl.ds(0, nx - 1)], agx_recv.at[level, 0])
-        drains.append((box.at[0, pl.ds(0, nz - 1)], agz_send.at[level]))
-        drains.append((box.at[pl.ds(0, nx - 1)], agx_send.at[level]))
-
     def broadcast(level):
-        if halves(level):
+        wait_bytes(from_leaf[level].at[pl.ds(0, nl - 1)], leaf_recv.at[level])
+        if not fast:
             broadcast_listed(level)
             return
-        wait_bytes(from_leaf[level].at[pl.ds(0, nl - 1)], leaf_recv.at[level])
         wanted = need[2 * level - 2 : 2 * level - 1, :]
         chosen = jnp.zeros((quarter, width), F32)
         for node in range(nl):
             chosen = jnp.where(wanted == float(node), from_leaf[level][node], chosen)
-        gather_plane(gathers[level], chosen, level)
+        gathers[level][blk] = chosen
+        gather_plane(gathers[level], level)
 
     def need_start():
         at = lax.broadcasted_iota(jnp.int32, (8, width), 0)
@@ -233,11 +260,13 @@
 
         def one(s, _):
             at = lax.rem(rows_ref[0, 0, s], nz)
-            if halves(level - 1):
-                node = slot_node[s] if level > 1 else 0
+            if level == 1:
+                panel = jnp.concatenate([box[h, at * nx + q] for q in range(nx) for h in range(2)], axis=0)
+            elif fast:
+                panel = jnp.concatenate([box[at * nx + q] for q in range(nx)], axis=0)
+            else:
+                node = slot_node[s]
                 panel = jnp.concatenate([box[h, q, at, node] for q in range(nx) for h in range(2)], axis=0)
-            else:
-                panel = jnp.concatenate([box[q, at] for q in range(nx)], axis=0)
             high, low = split(panel)
             both = jnp.concatenate([high, low], axis=0)
             got = jnp.dot(both, weights[s], preferred_element_type=F32)
@@ -247,7 +276,7 @@
 
         lax.fori_loop(0, slots, one, 0, unroll=4)
 
-        def column(c, _):
+        def column(c):
             total = jnp.zeros((nx * quarter, width), F32)
             for s in range(slots):
                 key = jnp.where(slot_level[s] == level - 1, cols_ref[0, 0, s], -1)
@@ -255,36 +284,33 @@
             for q in range(nx):
                 mass = total[q * quarter : (q + 1) * quarter]
                 part[q, c] = mass if level == 1 else part[q, c] + mass
-            return 0
-
-        lax.fori_loop(0, nz, column, 0)
+
+        def visit(dz, order):
+            c = z_peer(dz)
+            column(c)
+            for dx in order:
+                send(
+                    part.at[x_peer(dx), c], from_plane.at[level - 1, dz * nx + dx],
+                    part_send.at[level - 1], part_recv.at[level - 1], (leaf, c * nx + x_peer(dx)),
+                )
+
+        plane_loop(visit)
 
     def reduce(level):
         at = level - 1
-        for k in range(1, nx):
-            send(part.at[x_peer(k)], from_x.at[at, k - 1], rsx_send.at[at], rsx_recv.at[at], at_x(k))
-        if level == 1 and fast:
+        if level == 1:
             need_end()
-        wait_bytes(from_x.at[at], rsx_recv.at[at])
-        total = part[x]
-        for k in range(nx - 1):
-            total = total + from_x[at, k]
-        to_z[at] = total
-        for k in range(1, nz):
-            send(to_z.at[at, z_peer(k)], from_z.at[at, k - 1], rsz_send.at[at], rsz_recv.at[at], at_z(k))
-        wait_bytes(from_z.at[at], rsz_recv.at[at])
-        total = to_z[at, z]
-        for k in range(nz - 1):
-            total = total + from_z[at, k]
-        drains.append((from_z.at[at], rsz_send.at[at]))
+        wait_bytes(from_plane.at[at, pl.ds(1, nz * nx - 1)], part_recv.at[at])
+        total = part[x, z]
+        for k in range(1, nz * nx):
+            total = total + from_plane[at, k]
         return total
 
     def drain_part(level):
-        wait_bytes(from_x.at[level - 1], rsx_send.at[level - 1])
+        wait_bytes(from_plane.at[level - 1, pl.ds(1, nz * nx - 1)], part_send.at[level - 1])
 
     leaf_start(0)
-    if fast:
-        need_start()
+    need_start()
     copies[6].wait()
 
     def prepare(s, _):
@@ -294,7 +320,7 @@
         return 0
 
     lax.fori_loop(0, slots, prepare, 0, unroll=2)
-    broadcast(0)
+    broadcast_root()
     for level in range(1, LEVELS):
         if level > 1:
             drain_part(level - 1)
@@ -307,18 +333,17 @@
             leaf_start(level)
             broadcast(level)
 
-    gather_plane(final, mine[...], LEVELS - 1)
+    final[blk] = mine[...]
+    gather_plane(final, LEVELS - 1)
     for q in range(nx):
-        out_ref[:, pl.ds(q * quarter, quarter), :] = final[q]
-
-    if fast:
-        wait_bytes(flags.at[pl.ds(0, nl - 1)], need_recv.at[2])
-        flag = flags[0]
-        for node in range(1, nl):
-            flag = jnp.maximum(flag, flags[node])
-        flag_ref[...] = flag
-    else:
-        flag_ref[...] = jnp.zeros_like(flag_ref)
+        for c in range(nz):
+            out_ref[c, pl.ds(q * quarter, quarter), :] = final[c * nx + q]
+
+    wait_bytes(flags.at[pl.ds(0, nl - 1)], need_recv.at[2])
+    flag = flags[0]
+    for node in range(1, nl):
+        flag = jnp.maximum(flag, flags[node])
+    flag_ref[0, 0] = jnp.where(jnp.max(flag) > 0.5, 1, 0).astype(jnp.int32)
     drain_part(LEVELS - 1)
     for ref, sem in drains:
         wait_bytes(ref, sem)
@@ -339,16 +364,16 @@
     vmem = pltpu.VMEM
     smem = pltpu.SMEM
     whole = pl.BlockSpec(memory_space=pltpu.VMEM)
-    box = (nx, nz, quarter, width) if fast else (2, nx, nz, cap, half, width)
+    box = (nb, quarter, width) if fast else (2, nx, nz, cap, half, width)
     side = (nl, quarter, width) if fast else (nl, half, width)
     return pl.pallas_call(
         functools.partial(kernel, cap, nl, nz, nx, slots, quarter, width),
         out_shape=(
             jax.ShapeDtypeStruct((per_node, columns, width), F32),
-            jax.ShapeDtypeStruct((8, width), F32),
+            jax.ShapeDtypeStruct((1, 1), jnp.int32),
         ),
         in_specs=[hbm] * 7,
-        out_specs=(whole, whole),
+        out_specs=(whole, pl.BlockSpec(memory_space=pltpu.SMEM)),
         scratch_shapes=[
             smem(node_level.shape, jnp.int32),
             smem(block_rows.shape, jnp.int32),
@@ -360,17 +385,15 @@
             vmem((slots, width, 2 * width), BF16),
             vmem((slots, columns, width), F32),
             vmem((nx, nz, quarter, width), F32),
-            vmem((last, nx - 1, nz, quarter, width), F32),
-            vmem((last, nz, quarter, width), F32),
-            vmem((last, nz - 1, quarter, width), F32),
+            vmem((last, nb, quarter, width), F32),
             vmem((LEVELS, quarter, width), F32),
             vmem((nl, half, width), F32),
             vmem(side, F32),
             vmem(side, F32),
-            vmem((2, nx, nz, 1, half, width), F32),
+            vmem((2, nb, half, width), F32),
             vmem(box, F32),
             vmem(box, F32),
-            vmem((nx, nz, quarter, width), F32),
+            vmem((nb, quarter, width), F32),
             vmem((quarter, width), F32),
             vmem((8, width), F32),
             vmem((nz - 1, 8, width), F32),
@@ -385,8 +408,6 @@
             dma((last,)),
             dma((last,)),
             dma((last,)),
-            dma((last,)),
-            dma((last,)),
             dma((LEVELS,)),
             dma((LEVELS,)),
             dma((LEVELS,)),
@@ -410,7 +431,7 @@
     )
     solved, flag = call(0, *args)
     cap = lax.axis_size("leaf") - 3
-    solved = lax.cond(flag[0, 0] > 0.5, lambda: call(cap, *args)[0], lambda: solved)
+    solved = lax.cond(flag[0, 0] > 0, lambda: call(cap, *args)[0], lambda: solved)
     return jnp.swapaxes(solved, 1, 2)
 
 

time: 113 us -> 101 us (0.89)
  the two profiles are of different devices: /device:TPU:4 before, /device:TPU:1 now
where the time goes in v3:
time: 101 us; the launch traced here: 100 us
  Pallas kernels  98.1 us (97%)
  between operations  1.52 us (2%)
    pallas_call x1, Pallas kernels, call(): pl.pallas_call(functools.partial(kernel, cap, nl, nz, nx, slots, quarter,...  98.1 us

profile of v3, /device:TPU:1, one launch (start us, length us, event | category | flops | bytes accessed | tf_op | source)
XLA Modules:
  0.0 100.4 jit_solution(7618224706865544546)
XLA Ops:
  0.0 0.0 copy-start.3
  0.0 0.0 copy-start.5
  0.0 0.0 copy-start.4
  0.0 0.0 copy-start.1
  0.0 0.0 copy-start
  0.0 0.0 copy-start.2
  0.8 98.1 %tree_solve.1 = (f32[8,64,128]{2,1,0:T(8,128)S(1)}, s32[1,1]{1,0:T(1,128)}) custom-call(s32[16]{0:T(128)} %level_hbm.1, s32[1,1,32]{2,1,0:T(1,128)} %rows_hbm.1, s32[1,1,32]{2,1,0:T(1,128)} %cols_hbm.1, s32[1,1]{1,0:T(1,128)S(6)} %copy.11.count_hbm, f32[8,64,128]{2,1,0:T(8,128)} %bitcast.6, f32[8,128,128]{2,1,0:T(8,128)} %dinv_hbm.1, f32[32,128,128]{2,1,0:T(8,128)} %bitcast.4), custom_call_target="tpu_custom_call" | custom-call | tf_op jit(solution)/shard_map/tree_solve/pallas_call | solution.py:369
  99.6 0.0 copy-done.3
  99.6 0.0 copy-done.5
  99.6 0.0 copy-done.4
  99.6 0.0 copy-done.1
  99.6 0.0 copy-done
  99.6 0.0 copy-done.2
  99.7 0.7 copy.12
  (1 shorter events, 0.0 us)
Async XLA Ops:
  0.0 99.6 %copy-start.3 = (s32[16]{0:T(128)S(1)}, s32[16]{0:T(128)}, u32[]{:S(2)}) copy-start(s32[16]{0:T(128)} %level_hbm.1) | copy-start | bytes 196
  0.0 99.6 %copy-start.5 = (s32[1,1,32]{2,1,0:T(1,128)S(1)}, s32[1,1,32]{2,1,0:T(1,128)}, u32[]{:S(2)}) copy-start(s32[1,1,32]{2,1,0:T(1,128)} %cols_hbm.1) | copy-start | bytes 388
  0.0 99.6 %copy-start.4 = (s32[1,1,32]{2,1,0:T(1,128)S(1)}, s32[1,1,32]{2,1,0:T(1,128)}, u32[]{:S(2)}) copy-start(s32[1,1,32]{2,1,0:T(1,128)} %rows_hbm.1) | copy-start | bytes 388
  0.0 99.6 %copy-start.1 = (f32[8,128,128]{2,1,0:T(8,128)S(1)}, f32[8,128,128]{2,1,0:T(8,128)}, u32[]{:S(2)}) copy-start(f32[8,128,128]{2,1,0:T(8,128)} %dinv_hbm.1) | copy-start | bytes 1572868
  0.0 99.6 %copy-start = (f32[1,1,32,128,128]{4,3,2,1,0:T(8,128)S(1)}, f32[1,1,32,128,128]{4,3,2,1,0:T(8,128)}, u32[]{:S(2)}) copy-start(f32[1,1,32,128,128]{4,3,2,1,0:T(8,128)} %param.11) | copy-start | bytes 6291460
  0.0 99.6 %copy-start.2 = (f32[8,128,64]{1,2,0:T(8,128)S(1)}, f32[8,128,64]{1,2,0:T(8,128)}, u32[]{:S(2)}) copy-start(f32[8,128,64]{1,2,0:T(8,128)} %param.9) | copy-start | bytes 786436

commit v4 on v3

--- a/solution.py
+++ b/solution.py
@@ -8,6 +8,7 @@
 from jax.sharding import PartitionSpec as P
 
 LEVELS = 4
+UNROLL = 8
 VMEM_LIMIT = 60 * 1024 * 1024
 MESH = pl.DeviceIdType.MESH
 F32 = jnp.float32
@@ -24,7 +25,7 @@
     level_hbm, rows_hbm, cols_hbm, count_hbm, rhs_hbm, dinv_hbm, tiles_hbm,
     out_ref, flag_ref,
     level_ref, rows_ref, cols_ref, count_ref,
-    tiles, dinv, own_rhs, weights, prods, part, from_plane, piece, leaf0, leaf1, leaf2, gather0, gather1, gather2,
+    tiles, dinv, own_rhs, weights, panels, prods, part, from_plane, piece, leaf0, leaf1, leaf2, gather0, gather1, gather2,
     final, mine, need, need_z, need_x, flags, rank, names, slot_node, slot_level,
     local_sems, leaf_send, leaf_recv, part_send, part_recv, agz_send, agz_recv, agx_send, agx_recv,
     core_send, core_recv, need_send, need_recv,
@@ -258,23 +259,34 @@
     def products(level):
         box = gathers[level - 1]
 
+        listed = cap if level > 1 and not fast else 1
+
+        def arrange(c, _):
+            for node in range(listed):
+                for q in range(nx):
+                    if level == 1:
+                        panel = jnp.concatenate([box[h, c * nx + q] for h in range(2)], axis=0)
+                    elif fast:
+                        panel = box[c * nx + q]
+                    else:
+                        panel = jnp.concatenate([box[h, q, c, node] for h in range(2)], axis=0)
+                    high, low = split(panel)
+                    rows = pl.ds(q * quarter, quarter)
+                    panels[c * listed + node, rows, pl.ds(0, width)] = high
+                    panels[c * listed + node, rows, pl.ds(width, width)] = low
+            return 0
+
+        lax.fori_loop(0, nz, arrange, 0, unroll=True if listed == 1 else 1)
+
         def one(s, _):
             at = lax.rem(rows_ref[0, 0, s], nz)
-            if level == 1:
-                panel = jnp.concatenate([box[h, at * nx + q] for q in range(nx) for h in range(2)], axis=0)
-            elif fast:
-                panel = jnp.concatenate([box[at * nx + q] for q in range(nx)], axis=0)
-            else:
-                node = slot_node[s]
-                panel = jnp.concatenate([box[h, q, at, node] for q in range(nx) for h in range(2)], axis=0)
-            high, low = split(panel)
-            both = jnp.concatenate([high, low], axis=0)
-            got = jnp.dot(both, weights[s], preferred_element_type=F32)
-            n = nx * quarter
-            prods[s] = (got[:n, width:] + got[n:, :width]) + got[:n, :width]
+            if listed > 1:
+                at = at * listed + slot_node[s]
+            got = jnp.dot(panels[at], weights[s], preferred_element_type=F32)
+            prods[s] = got[:, width:] + got[:, :width]
             return 0
 
-        lax.fori_loop(0, slots, one, 0, unroll=4)
+        lax.fori_loop(0, slots, one, 0, unroll=UNROLL)
 
         def column(c):
             total = jnp.zeros((nx * quarter, width), F32)
@@ -315,8 +327,10 @@
 
     def prepare(s, _):
         high, low = split(tiles[s])
-        weights[s, :, :width] = high
-        weights[s, :, width:] = low
+        weights[s, :width, :width] = high
+        weights[s, :width, width:] = low
+        weights[s, width:, :width] = high
+        weights[s, width:, width:] = jnp.zeros_like(low)
         return 0
 
     lax.fori_loop(0, slots, prepare, 0, unroll=2)
@@ -382,7 +396,8 @@
             vmem((slots, width, width), F32),
             vmem((width, width), F32),
             vmem((quarter, width), F32),
-            vmem((slots, width, 2 * width), BF16),
+            vmem((slots, 2 * width, 2 * width), BF16),
+            vmem((nz * (1 if fast else cap), columns, 2 * width), BF16),
             vmem((slots, columns, width), F32),
             vmem((nx, nz, quarter, width), F32),
             vmem((last, nb, quarter, width), F32),

time: 101 us -> 98.6 us (0.976)
  Pallas kernels: 98.1 us -> 96.2 us
    pallas_call x1, Pallas kernels: 98.1 us -> 96.2 us  [call(): pl.pallas_call(functools.partial(kernel, cap, nl, nz, nx, slots, quarter,...]
where the time goes in v4:
time: 98.6 us; the launch traced here: 98.4 us
  Pallas kernels  96.2 us (98%)
  between operations  1.52 us (2%)
    pallas_call x1, Pallas kernels, call(): pl.pallas_call(functools.partial(kernel, cap, nl, nz, nx, slots, quarter,...  96.2 us

profile of v4, /device:TPU:1, one launch (start us, length us, event | category | flops | bytes accessed | tf_op | source)
XLA Modules:
  0.0 98.4 jit_solution(1876793881618779152)
XLA Ops:
  0.0 0.0 copy-start.3
  0.0 0.0 copy-start.5
  0.0 0.0 copy-start.4
  0.0 0.0 copy-start.1
  0.0 0.0 copy-start
  0.0 0.0 copy-start.2
  0.8 96.2 %tree_solve.1 = (f32[8,64,128]{2,1,0:T(8,128)S(1)}, s32[1,1]{1,0:T(1,128)}) custom-call(s32[16]{0:T(128)} %level_hbm.1, s32[1,1,32]{2,1,0:T(1,128)} %rows_hbm.1, s32[1,1,32]{2,1,0:T(1,128)} %cols_hbm.1, s32[1,1]{1,0:T(1,128)S(6)} %copy.11.count_hbm, f32[8,64,128]{2,1,0:T(8,128)} %bitcast.6, f32[8,128,128]{2,1,0:T(8,128)} %dinv_hbm.1, f32[32,128,128]{2,1,0:T(8,128)} %bitcast.4), custom_call_target="tpu_custom_call" | custom-call | tf_op jit(solution)/shard_map/tree_solve/pallas_call | solution.py:383
  97.6 0.0 copy-done.3
  97.7 0.0 copy-done.5
  97.7 0.0 copy-done.4
  97.7 0.0 copy-done.1
  97.7 0.0 copy-done
  97.7 0.0 copy-done.2
  97.7 0.7 copy.12
  (1 shorter events, 0.0 us)
Async XLA Ops:
  0.0 97.6 %copy-start.3 = (s32[16]{0:T(128)S(1)}, s32[16]{0:T(128)}, u32[]{:S(2)}) copy-start(s32[16]{0:T(128)} %level_hbm.1) | copy-start | bytes 196
  0.0 97.7 %copy-start.5 = (s32[1,1,32]{2,1,0:T(1,128)S(1)}, s32[1,1,32]{2,1,0:T(1,128)}, u32[]{:S(2)}) copy-start(s32[1,1,32]{2,1,0:T(1,128)} %cols_hbm.1) | copy-start | bytes 388
  0.0 97.7 %copy-start.4 = (s32[1,1,32]{2,1,0:T(1,128)S(1)}, s32[1,1,32]{2,1,0:T(1,128)}, u32[]{:S(2)}) copy-start(s32[1,1,32]{2,1,0:T(1,128)} %rows_hbm.1) | copy-start | bytes 388
  0.0 97.7 %copy-start.1 = (f32[8,128,128]{2,1,0:T(8,128)S(1)}, f32[8,128,128]{2,1,0:T(8,128)}, u32[]{:S(2)}) copy-start(f32[8,128,128]{2,1,0:T(8,128)} %dinv_hbm.1) | copy-start | bytes 1572868
  0.0 97.7 %copy-start = (f32[1,1,32,128,128]{4,3,2,1,0:T(8,128)S(1)}, f32[1,1,32,128,128]{4,3,2,1,0:T(8,128)}, u32[]{:S(2)}) copy-start(f32[1,1,32,128,128]{4,3,2,1,0:T(8,128)} %param.11) | copy-start | bytes 6291460
  0.0 97.7 %copy-start.2 = (f32[8,128,64]{1,2,0:T(8,128)S(1)}, f32[8,128,64]{1,2,0:T(8,128)}, u32[]{:S(2)}) copy-start(f32[8,128,64]{1,2,0:T(8,128)} %param.9) | copy-start | bytes 786436

commit v5 on v4

--- a/solution.py
+++ b/solution.py
@@ -153,7 +153,7 @@
 
     def far_first(i, n):
         step = lax.div(i + 1, 2)
-        return jnp.where(lax.rem(i, 2) == 1, n // 2 - step, n // 2 + step)
+        return jnp.where(lax.rem(i, 2) == 1, lax.rem(n // 2 + step, n), n // 2 - step)
 
     def plane_loop(visit):
         order = [nx // 2 + (-1) ** i * ((i + 1) // 2) for i in range(nx)]
@@ -171,7 +171,12 @@
             for dx in order:
                 send(own, box_at, send_sem, recv_sem, (leaf, z_peer(dz) * nx + x_peer(dx)))
 
-        plane_loop(visit)
+        def far(n, d):
+            return min(d, n - d)
+
+        pairs = [(a, b) for a in range(nz) for b in range(nx) if a or b]
+        for dz, dx in sorted(pairs, key=lambda p: (-far(nz, p[0]) - far(nx, p[1]), -far(nz, p[0]), -p[0])):
+            visit(dz, [dx])
 
     def gather_plane(box, level):
         own = box.at[blk]

time: 98.6 us -> 97.4 us (0.988)
  Pallas kernels: 96.2 us -> 95 us
    pallas_call x1, Pallas kernels: 96.2 us -> 95 us  [call(): pl.pallas_call(functools.partial(kernel, cap, nl, nz, nx, slots, quarter,...]
where the time goes in v5:
time: 97.4 us; the launch traced here: 97.2 us
  Pallas kernels  95 us (98%)
  between operations  1.52 us (2%)
    pallas_call x1, Pallas kernels, call(): pl.pallas_call(functools.partial(kernel, cap, nl, nz, nx, slots, quarter,...  95 us

profile of v5, /device:TPU:1, one launch (start us, length us, event | category | flops | bytes accessed | tf_op | source)
XLA Modules:
  0.0 97.2 jit_solution(9500332883521653429)
XLA Ops:
  0.0 0.0 copy-start.3
  0.0 0.0 copy-start.5
  0.0 0.0 copy-start.4
  0.0 0.0 copy-start.1
  0.0 0.0 copy-start
  0.0 0.0 copy-start.2
  0.8 95.0 %tree_solve.1 = (f32[8,64,128]{2,1,0:T(8,128)S(1)}, s32[1,1]{1,0:T(1,128)}) custom-call(s32[16]{0:T(128)} %level_hbm.1, s32[1,1,32]{2,1,0:T(1,128)} %rows_hbm.1, s32[1,1,32]{2,1,0:T(1,128)} %cols_hbm.1, s32[1,1]{1,0:T(1,128)S(6)} %copy.11.count_hbm, f32[8,64,128]{2,1,0:T(8,128)} %bitcast.6, f32[8,128,128]{2,1,0:T(8,128)} %dinv_hbm.1, f32[32,128,128]{2,1,0:T(8,128)} %bitcast.4), custom_call_target="tpu_custom_call" | custom-call | tf_op jit(solution)/shard_map/tree_solve/pallas_call | solution.py:388
  96.5 0.0 copy-done.3
  96.5 0.0 copy-done.5
  96.5 0.0 copy-done.4
  96.5 0.0 copy-done.1
  96.5 0.0 copy-done
  96.5 0.0 copy-done.2
  96.5 0.7 copy.12
  (1 shorter events, 0.0 us)
Async XLA Ops:
  0.0 96.5 %copy-start.3 = (s32[16]{0:T(128)S(1)}, s32[16]{0:T(128)}, u32[]{:S(2)}) copy-start(s32[16]{0:T(128)} %level_hbm.1) | copy-start | bytes 196
  0.0 96.5 %copy-start.5 = (s32[1,1,32]{2,1,0:T(1,128)S(1)}, s32[1,1,32]{2,1,0:T(1,128)}, u32[]{:S(2)}) copy-start(s32[1,1,32]{2,1,0:T(1,128)} %cols_hbm.1) | copy-start | bytes 388
  0.0 96.5 %copy-start.4 = (s32[1,1,32]{2,1,0:T(1,128)S(1)}, s32[1,1,32]{2,1,0:T(1,128)}, u32[]{:S(2)}) copy-start(s32[1,1,32]{2,1,0:T(1,128)} %rows_hbm.1) | copy-start | bytes 388
  0.0 96.5 %copy-start.1 = (f32[8,128,128]{2,1,0:T(8,128)S(1)}, f32[8,128,128]{2,1,0:T(8,128)}, u32[]{:S(2)}) copy-start(f32[8,128,128]{2,1,0:T(8,128)} %dinv_hbm.1) | copy-start | bytes 1572868
  0.0 96.5 %copy-start = (f32[1,1,32,128,128]{4,3,2,1,0:T(8,128)S(1)}, f32[1,1,32,128,128]{4,3,2,1,0:T(8,128)}, u32[]{:S(2)}) copy-start(f32[1,1,32,128,128]{4,3,2,1,0:T(8,128)} %param.11) | copy-start | bytes 6291460
  0.0 96.5 %copy-start.2 = (f32[8,128,64]{1,2,0:T(8,128)S(1)}, f32[8,128,64]{1,2,0:T(8,128)}, u32[]{:S(2)}) copy-start(f32[8,128,64]{1,2,0:T(8,128)} %param.9) | copy-start | bytes 786436

commit v6 on v5

--- a/solution.py
+++ b/solution.py
@@ -25,7 +25,7 @@
     level_hbm, rows_hbm, cols_hbm, count_hbm, rhs_hbm, dinv_hbm, tiles_hbm,
     out_ref, flag_ref,
     level_ref, rows_ref, cols_ref, count_ref,
-    tiles, dinv, own_rhs, weights, panels, prods, part, from_plane, piece, leaf0, leaf1, leaf2, gather0, gather1, gather2,
+    tiles, dinv, inverse, own_rhs, weights, panels, prods, part, from_plane, piece, leaf0, leaf1, leaf2, gather0, gather1, gather2,
     final, mine, need, need_z, need_x, flags, rank, names, slot_node, slot_level,
     local_sems, leaf_send, leaf_recv, part_send, part_recv, agz_send, agz_recv, agx_send, agx_recv,
     core_send, core_recv, need_send, need_recv,
@@ -74,13 +74,20 @@
     for copy in copies:
         copy.start()
 
+    def fill(ref, matrix):
+        high, low = split(matrix)
+        ref[:width, :width] = high
+        ref[:width, width:] = low
+        ref[width:, :width] = high
+        ref[width:, width:] = jnp.zeros_like(low)
+
     def solve(summed):
-        return lax.dot_general(
-            own_rhs[...] - summed, dinv[...], (((1,), (1,)), ((), ())),
-            precision=lax.Precision.HIGHEST, preferred_element_type=F32,
-        )
+        both = jnp.concatenate(split(own_rhs[...] - summed), axis=1)
+        got = jnp.dot(both, inverse[...], preferred_element_type=F32)
+        return got[:, width:] + got[:, :width]
 
     copies[0].wait()
+    fill(inverse, dinv[...].T)
     copies[1].wait()
     piece[0] = solve(jnp.zeros((quarter, width), F32))
     mine[...] = piece[0]
@@ -178,9 +185,11 @@
         for dz, dx in sorted(pairs, key=lambda p: (-far(nz, p[0]) - far(nx, p[1]), -far(nz, p[0]), -p[0])):
             visit(dz, [dx])
 
-    def gather_plane(box, level):
+    def gather_plane(box, level, meanwhile=None):
         own = box.at[blk]
         send_all(own, own, agz_send.at[level], agz_recv.at[level])
+        if meanwhile:
+            meanwhile()
         others = box.at[pl.ds(0, nz * nx - 1)]
         wait_bytes(others, agz_recv.at[level])
         drains.append((others, agz_send.at[level]))
@@ -188,10 +197,10 @@
     def broadcast_root():
         box = gather0
         wait_bytes(leaf0.at[pl.ds(0, nl - 1)], leaf_recv.at[0])
-        need_across()
+        wait_bytes(need_z, need_recv.at[0])
         box[core, blk] = leaf0[names[0]]
         side = box.at[core]
-        gather_plane(side, 0)
+        gather_plane(side, 0, need_across)
         send(side, side, core_send.at[0], core_recv.at[0], sibling)
         wait_bytes(side, core_recv.at[0])
         drains.append((side, core_send.at[0]))
@@ -239,7 +248,6 @@
             send(need, need_z.at[k - 1], need_send.at[0], need_recv.at[0], at_z(k))
 
     def need_across():
-        wait_bytes(need_z, need_recv.at[0])
         wait_bytes(need_z, need_send.at[0])
         tile = need[...]
         for k in range(nz - 1):
@@ -400,6 +408,7 @@
             smem(block_count.shape, jnp.int32),
             vmem((slots, width, width), F32),
             vmem((width, width), F32),
+            vmem((2 * width, 2 * width), BF16),
             vmem((quarter, width), F32),
             vmem((slots, 2 * width, 2 * width), BF16),
             vmem((nz * (1 if fast else cap), columns, 2 * width), BF16),

time: 97.4 us -> 96.7 us (level)
  Pallas kernels: 95 us -> 93.7 us
    pallas_call x1, Pallas kernels: 95 us -> 93.7 us  [call(): pl.pallas_call(functools.partial(kernel, cap, nl, nz, nx, slots, quarter,...]
where the time goes in v6:
time: 96.7 us; the launch traced here: 96 us
  Pallas kernels  93.7 us (97%)
  between operations  1.52 us (2%)
    pallas_call x1, Pallas kernels, call(): pl.pallas_call(functools.partial(kernel, cap, nl, nz, nx, slots, quarter,...  93.7 us

profile of v6, /device:TPU:1, one launch (start us, length us, event | category | flops | bytes accessed | tf_op | source)
XLA Modules:
  0.0 96.0 jit_solution(17312309568878085726)
XLA Ops:
  0.0 0.0 copy-start.3
  0.0 0.0 copy-start.5
  0.0 0.0 copy-start.4
  0.0 0.0 copy-start.1
  0.0 0.0 copy-start
  0.0 0.0 copy-start.2
  0.8 93.7 %tree_solve.1 = (f32[8,64,128]{2,1,0:T(8,128)S(1)}, s32[1,1]{1,0:T(1,128)}) custom-call(s32[16]{0:T(128)} %level_hbm.1, s32[1,1,32]{2,1,0:T(1,128)} %rows_hbm.1, s32[1,1,32]{2,1,0:T(1,128)} %cols_hbm.1, s32[1,1]{1,0:T(1,128)S(6)} %copy.11.count_hbm, f32[8,64,128]{2,1,0:T(8,128)} %bitcast.6, f32[8,128,128]{2,1,0:T(8,128)} %dinv_hbm.1, f32[32,128,128]{2,1,0:T(8,128)} %bitcast.4), custom_call_target="tpu_custom_call" | custom-call | tf_op jit(solution)/shard_map/tree_solve/pallas_call | solution.py:396
  95.2 0.0 copy-done.3
  95.2 0.0 copy-done.5
  95.2 0.0 copy-done.4
  95.2 0.0 copy-done.1
  95.2 0.0 copy-done
  95.2 0.0 copy-done.2
  95.3 0.7 copy.12
  (1 shorter events, 0.0 us)
Async XLA Ops:
  0.0 95.2 %copy-start.3 = (s32[16]{0:T(128)S(1)}, s32[16]{0:T(128)}, u32[]{:S(2)}) copy-start(s32[16]{0:T(128)} %level_hbm.1) | copy-start | bytes 196
  0.0 95.2 %copy-start.5 = (s32[1,1,32]{2,1,0:T(1,128)S(1)}, s32[1,1,32]{2,1,0:T(1,128)}, u32[]{:S(2)}) copy-start(s32[1,1,32]{2,1,0:T(1,128)} %cols_hbm.1) | copy-start | bytes 388
  0.0 95.2 %copy-start.4 = (s32[1,1,32]{2,1,0:T(1,128)S(1)}, s32[1,1,32]{2,1,0:T(1,128)}, u32[]{:S(2)}) copy-start(s32[1,1,32]{2,1,0:T(1,128)} %rows_hbm.1) | copy-start | bytes 388
  0.0 95.2 %copy-start.1 = (f32[8,128,128]{2,1,0:T(8,128)S(1)}, f32[8,128,128]{2,1,0:T(8,128)}, u32[]{:S(2)}) copy-start(f32[8,128,128]{2,1,0:T(8,128)} %dinv_hbm.1) | copy-start | bytes 1572868
  0.0 95.2 %copy-start = (f32[1,1,32,128,128]{4,3,2,1,0:T(8,128)S(1)}, f32[1,1,32,128,128]{4,3,2,1,0:T(8,128)}, u32[]{:S(2)}) copy-start(f32[1,1,32,128,128]{4,3,2,1,0:T(8,128)} %param.11) | copy-start | bytes 6291460
  0.0 95.2 %copy-start.2 = (f32[8,128,64]{1,2,0:T(8,128)S(1)}, f32[8,128,64]{1,2,0:T(8,128)}, u32[]{:S(2)}) copy-start(f32[8,128,64]{1,2,0:T(8,128)} %param.9) | copy-start | bytes 786436
